TPU v7x, 256 devices: a whole 4x4x8 slice. The times are simulated.
256 devices in a mesh: grp: 8 (over y, x_hi), row: 32 (over z, x_lo, core).
Axes of the slice: x: 4 (x_hi: 2, x_lo: 2; x = x_hi * 2 + x_lo), y: 4, z: 8, core: 2. Of those that a mesh axis runs over, the one named last changes fastest.
Arguments:
- features: float32 [32768, 256], P(('grp', 'row')), may hold values from -6 to 6
- adjacency_tiles: float32 [128, 8, 6, 256, 256], P('row', 'grp'), may hold values from -0.078125 to 0.078125
- tile_cols: int32 [128, 8, 6], P('row', 'grp'), may hold values from 0 to 15, as said below
- tile_count: int32 [128, 8], P('row', 'grp'), may hold values from 1 to 6, as said below
- weight: float32 [256, 256], replicated, may hold values from -0.375 to 0.375
- layer_bias: float32 [256], replicated, may hold values from -3 to 3
- cotangent: float32 [32768, 256], P('row'), may hold values from -6 to 6
Outputs:
- hidden_out: float32 [32768, 256], P('row')
- grad_features: float32 [32768, 256], P(('grp', 'row'))
- grad_weight: float32 [256, 256], replicated
- grad_bias: float32 [256], replicated
Inputs may be any that keep to these rules, and one draw needn't show every extreme that they name: `tile_cols`: for each block row and column range the 6 slots name distinct column blocks. `tile_count`: in every column range some block row has all 6 slots live.
All inputs are finite; a program needn't handle non-finite values.
Results may differ from a plain program's by a relative error of at most 0.0003.
Values sent between devices are 32-bit elements; how exact they have to be, the bound alone decides.
A program may use at most 128 MiB of HBM per device.

v0:
```python
import jax
import jax.numpy as jnp
from jax import lax
from jax.sharding import PartitionSpec as P


def activate(summed, upstream, weight, layer_bias):
    highest = lax.Precision.HIGHEST
    preact = jnp.dot(summed, weight, precision=highest) + layer_bias
    sigma = jax.nn.sigmoid(preact)
    grad_pre = upstream * sigma * (1.0 + preact * (1.0 - sigma))
    return (preact * sigma, grad_pre)


def on_device(features, adjacency_tiles, tile_cols, tile_count, weight, layer_bias, cotangent):
    highest = lax.Precision.HIGHEST
    block_rows, _, slot_count, tile_size, _ = adjacency_tiles.shape
    panel = lax.all_gather(features, "row", axis=0, tiled=True)
    width = panel.shape[1]
    blocks = panel.shape[0] // tile_size
    slots = lax.broadcasted_iota(jnp.int32, (block_rows, slot_count), 1)
    live = (slots < tile_count).astype(jnp.float32)
    block_ids = lax.broadcasted_iota(jnp.int32, (block_rows, slot_count, blocks), 2)
    picks = (tile_cols[:, 0, :, None] == block_ids).astype(jnp.float32) * live[:, :, None]
    local_tiles = adjacency_tiles[:, 0]
    chosen = jnp.einsum(
        "btc,cjf->btjf", picks, panel.reshape(blocks, tile_size, width), precision=highest
    )
    partial_rows = jnp.einsum("btij,btjf->bif", local_tiles, chosen, precision=highest).reshape(
        block_rows * tile_size, width
    )
    scaling = 1.0 / float(block_rows * tile_size * lax.axis_size("row")) ** 0.5
    summed = lax.psum(partial_rows, "grp")
    layer_out, grad_pre = activate(summed, cotangent, weight, layer_bias)
    weight_term = jnp.dot(summed.T, grad_pre, precision=highest) * scaling
    bias_term = jnp.sum(grad_pre, axis=0) * scaling
    grad_weight, grad_bias = lax.psum((weight_term, bias_term), "row")
    backward = jnp.dot(grad_pre, weight.T, precision=highest)
    spread = jnp.einsum(
        "btij,bif->btjf",
        local_tiles,
        backward.reshape(block_rows, tile_size, width),
        precision=highest,
    )
    grad_panel = jnp.einsum("btc,btjf->cjf", picks, spread, precision=highest).reshape(
        blocks * tile_size, width
    )
    grad_owned = lax.psum_scatter(grad_panel, "row", scatter_dimension=0, tiled=True)
    return (layer_out, grad_owned, grad_weight, grad_bias)


def solution(mesh):
    return jax.shard_map(
        on_device,
        mesh=mesh,
        in_specs=(
            P(("grp", "row"), None),
            P("row", "grp", None, None, None),
            P("row", "grp", None),
            P("row", "grp"),
            P(),
            P(),
            P("row", None),
        ),
        out_specs=(P("row", None), P(("grp", "row"), None), P(), P()),
        check_vma=False,
    )
```

profile of v0, /device:TPU:16, one launch (start us, length us, event | category | flops | bytes accessed | tf_op | source)
XLA Modules:
  0.0 565.5 jit_solution(5792356195475707266)
XLA Ops:
  7.2 0.0 copy-start
  7.2 0.0 all-gather.2.cloned.1.call-start
  7.2 0.0 slice-start
  7.2 0.7 all-gather.2.cloned.1.call-update
  7.9 0.0 all-reduce.3.cloned.1.call-start
  8.0 0.7 fusion.19
  8.7 70.5 %all-gather.2.cloned.1.call-done = f32[4096,256]{1,0:T(8,128)} async-done(((f32[128,256]{1,0:T(8,128)}), f32[4096,256]{1,0:T(8,128)}) %all-gather.2.cloned.1.call-update) | async-done | bytes 4194320 | tf_op jit(solution)/shard_map/all_gather | solution.py:18
  79.2 11.8 %fusion.7 = f32[4,6,256,256]{3,1,2,0:T(8,128)S(1)} fusion(f32[16,256,256,1]{2,1,0,3:T(8,128)} %bitcast.47, f32[4,6]{1,0:T(4,128)S(1)} %fusion.19, s32[4,6]{1,0:T(4,128)} %bitcast.50), kind=kOutput, calls=%fused_computation.7 | convolution fusion | flops 301990656 | bytes 10485952 | tf_op jit(solution)/shard_map/btc,cjf->btjf/dot_general | solution.py:26
  91.0 0.0 slice-done
  91.0 0.0 copy-start.3
  91.1 0.0 copy-start.4
  91.1 9.5 %fusion.4 = f32[4,256,256,1]{1,2,3,0:T(8,128)} fusion(f32[4,1,6,256,256]{4,3,2,1,0:T(8,128)S(1)} %bitcast.45, f32[4,6,256,256]{3,1,2,0:T(8,128)S(1)} %fusion.7), kind=kOutput, calls=%fused_computation.4 | convolution fusion | flops 4831838208 | bytes 13631488 | tf_op jit(solution)/shard_map/btij,btjf->bif/dot_general | solution.py:29
  100.6 0.0 all-reduce.3.cloned.1.call-update
  100.6 0.3 all-reduce.5.cloned.1.call-start
  100.9 93.2 %all-reduce.3.cloned.1.call-done = f32[1024,256]{1,0:T(8,128)} async-done(((f32[1024,256]{1,0:T(8,128)}), f32[1024,256]{1,0:T(8,128)}) %all-reduce.3.cloned.1.call-update) | async-done | bytes 1048592 | tf_op jit(solution)/shard_map/psum | solution.py:33
  194.0 0.0 copy-done
  194.0 3.6 fusion.22
  197.6 1.0 fusion.23
  198.6 0.0 copy-done.1
  198.6 2.5 convolution_multiply_fusion
  201.2 0.0 all-reduce.5.cloned.1.call-update
  201.2 0.0 reduce-scatter.2.cloned.1.call-start
  201.2 11.8 %fusion.2 = f32[4,256,6,256]{3,1,2,0:T(8,128)} fusion(f32[4,256,256,1]{2,1,3,0:T(8,128)S(1)} %bitcast.48, f32[4,1,6,256,256]{4,3,2,1,0:T(8,128)} %param.8), kind=kOutput, calls=%fused_computation.2 | convolution fusion | flops 4831838208 | bytes 13631488 | tf_op jit(solution)/shard_map/btij,bif->btjf/dot_general | solution.py:39
  213.1 9.4 %copy.17 = f32[4,256,6,256]{1,2,0,3:T(8,128)} copy(f32[4,256,6,256]{3,1,2,0:T(8,128)} %fusion.2) | data formatting | bytes 12582912 | tf_op jit(solution)/shard_map/btij,bif->btjf/dot_general | solution.py:39
  222.5 0.0 copy-done.2
  222.5 9.3 %fusion.9 = f32[16,256,256]{2,0,1:T(8,128)S(1)} fusion(f32[4,256,6,256]{1,2,0,3:T(8,128)} %copy.17, f32[4,6]{1,0:T(4,128)S(1)} %fusion.19, s32[4,6]{1,0:T(4,128)S(1)} %bitcast.51), kind=kOutput, calls=%fused_computation.9 | convolution fusion | flops 301990656 | bytes 10485952 | tf_op jit(solution)/shard_map/btc,btjf->cjf/dot_general | solution.py:45
  231.8 4.4 copy.11
  236.1 0.0 reduce-scatter.2.cloned.1.call-update
  236.2 53.5 %psum.23 = f32[256]{0:T(256)} all-reduce(f32[256]{0:T(256)S(1)} %broadcast_multiply_fusion), channel_id=1, replica_groups=mesh['grp'=8,'row'=32] {'row'}, use_global_device_ids=true, to_apply=%region_4.0 | all-reduce | flops 256 | bytes 2048 | tf_op jit(solution)/shard_map/psum | solution.py:37
  289.7 138.6 %all-reduce.5.cloned.1.call-done = f32[256,256]{1,0:T(8,128)} async-done(((f32[256,256]{1,0:T(8,128)}), f32[256,256]{1,0:T(8,128)}) %all-reduce.5.cloned.1.call-update) | async-done | bytes 262160 | tf_op jit(solution)/shard_map/psum | solution.py:37
  428.3 128.9 %reduce-scatter.2.cloned.1.call-done = f32[128,256]{1,0:T(8,128)} async-done(((f32[4096,256]{1,0:T(8,128)}), f32[128,256]{1,0:T(8,128)}) %reduce-scatter.2.cloned.1.call-update) | async-done | bytes 131088 | tf_op jit(solution)/shard_map/reduce_scatter | solution.py:48
  557.3 1.7 copy.25
  (8 shorter events, 0.0 us)
Async XLA Ops:
  7.2 186.9 %copy-start = (f32[256,256]{1,0:T(8,128)S(1)}, f32[256,256]{1,0:T(8,128)}, u32[]{:S(2)}) copy-start(f32[256,256]{1,0:T(8,128)} %param.11) | copy-start | bytes 786436
  7.2 72.0 %all-gather.2.cloned.1.call-start = ((), (), s32[]{:S(2)}) async-start(), calls=%async_computation.1 | async-start | bytes 4325376 | tf_op jit(solution)/shard_map/all_gather | solution.py:18
  7.2 83.8 %slice-start = ((s8[6291456]{0:T(1024)(128)(4,1)}), s8[2097152]{0:T(1024)(128)(4,1)S(1)}, s32[]{:S(2)}) async-start(s8[6291456]{0:T(1024)(128)(4,1)} %bitcast.44), calls=%async_computation.5 | async-start | bytes 4194304
  7.9 186.1 %all-reduce.3.cloned.1.call-start = ((), (), s32[]{:S(2)}) async-start(), calls=%async_computation.2 | async-start | bytes 2097152 | tf_op jit(solution)/shard_map/psum | solution.py:33
  79.2 11.9 %slice-start.1 = ((s8[6291456]{0:T(1024)(128)(4,1)}), s8[4194304]{0:T(1024)(128)(4,1)S(1)}, s32[]{:S(2)}) async-start(s8[6291456]{0:T(1024)(128)(4,1)} %bitcast.44), calls=%async_computation.6 | async-start | bytes 8388608
  91.0 103.0 %copy-start.3 = (f32[1024,256]{1,0:T(8,128)S(1)}, f32[1024,256]{1,0:T(8,128)}, u32[]{:S(2)}) copy-start(f32[1024,256]{1,0:T(8,128)} %param.13) | copy-start | bytes 3145732
  91.1 103.0 %copy-start.4 = (f32[256]{0:T(256)S(1)}, f32[256]{0:T(256)}, u32[]{:S(2)}) copy-start(f32[256]{0:T(256)} %param.12) | copy-start | bytes 3076
  100.6 327.7 %all-reduce.5.cloned.1.call-start = ((), (), s32[]{:S(2)}) async-start(), calls=%async_computation.4 | async-start | bytes 524288 | tf_op jit(solution)/shard_map/psum | solution.py:37
  194.0 4.6 copy-start.1
  201.2 356.1 %reduce-scatter.2.cloned.1.call-start = ((), (), s32[]{:S(2)}) async-start(), calls=%async_computation.3 | async-start | bytes 4325376 | tf_op jit(solution)/shard_map/reduce_scatter | solution.py:48
  213.1 9.4 %copy-start.2 = (s32[4,1,6]{2,1,0:T(1,128)S(1)}, s32[4,1,6]{2,1,0:T(1,128)}, u32[]{:S(2)}) copy-start(s32[4,1,6]{2,1,0:T(1,128)} %param.9) | copy-start | bytes 292
Sparse Core Ops, SparseCore 0:
  9.8 69.2 all-gather.1
  100.7 93.2 all-reduce.2
  201.3 226.9 all-reduce.4
  431.3 125.9 reduce-scatter.1
where the time goes:
time: 566 us; the launch traced here: 565 us
  waiting for transfers between devices  432 us (76%)
  blocking collectives  53.5 us (9%)
  matrix products  49.5 us (9%)
  local copies, waits for them, and re-layouts  15.5 us (3%)
  between operations  13.9 us (2%)
    psum x1, waiting for transfers between devices, on_device(): grad_weight, grad_bias = lax.psum((weight_term, bias_term), 'row')  139 us
    reduce_scatter x1, waiting for transfers between devices, on_device(): lax.psum_scatter(grad_panel, 'row', scatter_dimension=0, tiled=True)  129 us
    psum x1, waiting for transfers between devices, on_device(): summed = lax.psum(partial_rows, 'grp')  93.2 us
    all_gather x1, waiting for transfers between devices, on_device(): panel = lax.all_gather(features, 'row', axis=0, tiled=True)  70.5 us
    psum x1, blocking collectives, on_device(): grad_weight, grad_bias = lax.psum((weight_term, bias_term), 'row')  53.5 us
    dot_general x1, matrix products, on_device(): jnp.einsum('btc,cjf->btjf', picks, panel.reshape(blocks, tile_size, width...  11.8 us
    dot_general x1, matrix products, on_device(): jnp.einsum('btij,bif->btjf', local_tiles, backward.reshape(block_rows, ti...  11.8 us
  transfers between devices with their start and end apart: 4, of which 4 were waited for; matrix products, arithmetic and copies ran while one was open for 6% of the time, Pallas kernels for 0%

commit v1 on v0

--- a/solution.py
+++ b/solution.py
@@ -2,6 +2,12 @@
 import jax.numpy as jnp
 from jax import lax
 from jax.sharding import PartitionSpec as P
+from jax.lax import all_gather
+
+
+def open_cube(row_data):
+    view_out = all_gather(row_data, "grp").sum(axis=0)
+    return view_out
 
 
 def activate(summed, upstream, weight, layer_bias):
@@ -30,7 +36,7 @@
         block_rows * tile_size, width
     )
     scaling = 1.0 / float(block_rows * tile_size * lax.axis_size("row")) ** 0.5
-    summed = lax.psum(partial_rows, "grp")
+    summed = open_cube(partial_rows)
     layer_out, grad_pre = activate(summed, cotangent, weight, layer_bias)
     weight_term = jnp.dot(summed.T, grad_pre, precision=highest) * scaling
     bias_term = jnp.sum(grad_pre, axis=0) * scaling

time: 566 us -> 584 us (1.032)
  waiting for transfers between devices: 432 us -> 445 us
    all_gather x0 -> x1, waiting for transfers between devices: none -> 110 us  [open_cube(): view_out = all_gather(row_data, 'grp').sum(axis=0)]
    psum x1 -> x0, waiting for transfers between devices: 93.2 us -> none  [on_device(): summed = lax.psum(partial_rows, 'grp')]
where the time goes in v1:
time: 584 us
  waiting for transfers between devices  445 us (76%)
  blocking collectives  55.6 us (10%)
  matrix products  48.3 us (8%)
  local copies, waits for them, and re-layouts  15.5 us (3%)
  between operations  13.9 us (2%)
    psum x1, waiting for transfers between devices, on_device(): grad_weight, grad_bias = lax.psum((weight_term, bias_term), 'row')  135 us
    reduce_scatter x1, waiting for transfers between devices, on_device(): lax.psum_scatter(grad_panel, 'row', scatter_dimension=0, tiled=True)  129 us
    all_gather x1, waiting for transfers between devices, open_cube(): view_out = all_gather(row_data, 'grp').sum(axis=0)  110 us
    all_gather x1, waiting for transfers between devices, on_device(): panel = lax.all_gather(features, 'row', axis=0, tiled=True)  70.5 us
    psum x1, blocking collectives, on_device(): grad_weight, grad_bias = lax.psum((weight_term, bias_term), 'row')  55.6 us
    dot_general x1, matrix products, on_device(): jnp.einsum('btij,bif->btjf', local_tiles, backward.reshape(block_rows, ti...  11.9 us
    dot_general x1, matrix products, on_device(): jnp.einsum('btc,cjf->btjf', picks, panel.reshape(blocks, tile_size, width...  11.8 us
  transfers between devices with their start and end apart: 4, of which 4 were waited for; matrix products, arithmetic and copies ran while one was open for 6% of the time, Pallas kernels for 0%

profile of v1, /device:TPU:16, one launch (start us, length us, event | category | flops | bytes accessed | tf_op | source)
XLA Modules:
  0.0 583.7 jit_solution(18388002900889105483)
XLA Ops:
  7.2 0.0 copy-start
  7.2 0.0 all-gather.3.cloned.1.call-start
  7.2 0.0 slice-start
  7.2 0.7 all-gather.3.cloned.1.call-update
  7.9 0.0 all-gather.5.cloned.1.call-start
  8.0 0.7 fusion.18
  8.7 70.5 %all-gather.3.cloned.1.call-done = f32[4096,256]{1,0:T(8,128)} async-done(((f32[128,256]{1,0:T(8,128)}), f32[4096,256]{1,0:T(8,128)}) %all-gather.3.cloned.1.call-update) | async-done | bytes 4194320 | tf_op jit(solution)/shard_map/all_gather | solution.py:24
  79.2 11.8 %fusion.5 = f32[4,6,256,256]{3,1,2,0:T(8,128)S(1)} fusion(f32[16,256,256]{2,1,0:T(8,128)} %bitcast.48, f32[4,6]{1,0:T(4,128)S(1)} %fusion.18, s32[4,6]{1,0:T(4,128)} %bitcast.51), kind=kOutput, calls=%fused_computation.5 | convolution fusion | flops 301990656 | bytes 10485952 | tf_op jit(solution)/shard_map/btc,cjf->btjf/dot_general | solution.py:32
  91.0 0.0 slice-done
  91.0 0.0 slice-done.1
  91.0 9.5 %fusion.2 = f32[4,256,256,1]{1,2,3,0:T(8,128)} fusion(f32[4,1,6,256,256]{4,3,2,1,0:T(8,128)S(1)} %bitcast.46, f32[4,6,256,256]{3,1,2,0:T(8,128)S(1)} %fusion.5), kind=kOutput, calls=%fused_computation.2 | convolution fusion | flops 4831838208 | bytes 13631488 | tf_op jit(solution)/shard_map/btij,btjf->bif/dot_general | solution.py:35
  100.6 0.0 all-gather.5.cloned.1.call-update
  100.6 0.3 all-reduce.2.cloned.1.call-start
  100.9 109.9 %all-gather.5.cloned.1.call-done = f32[8,1024,256]{2,1,0:T(8,128)} async-done(((f32[1,1024,256]{2,1,0:T(8,128)}), f32[8,1024,256]{2,1,0:T(8,128)}) %all-gather.5.cloned.1.call-update) | async-done | bytes 8388624 | tf_op jit(solution)/shard_map/all_gather | solution.py:9
  210.7 4.1 reduce_sum.18
  214.8 0.0 copy-done
  214.8 0.0 copy-done.2
  214.8 0.0 copy-done.3
  214.8 2.3 fusion.21
  217.1 2.5 convolution_multiply_fusion
  219.6 1.0 fusion.22
  220.6 0.0 all-reduce.2.cloned.1.call-update
  220.7 0.3 reduce-scatter.2.cloned.1.call-start
  221.0 11.9 %fusion.8 = f32[4,6,256,256]{2,3,1,0:T(8,128)} fusion(f32[4,256,256,1]{2,1,3,0:T(8,128)S(1)} %bitcast.50, f32[4,1,6,256,256]{4,3,2,1,0:T(8,128)} %param.8), kind=kOutput, calls=%fused_computation.8 | convolution fusion | flops 4831838208 | bytes 13631488 | tf_op jit(solution)/shard_map/btij,bif->btjf/dot_general | solution.py:45
  232.8 9.4 %copy.19 = f32[4,6,256,256]{3,1,0,2:T(8,128)} copy(f32[4,6,256,256]{2,3,1,0:T(8,128)} %fusion.8) | data formatting | bytes 12582912 | tf_op jit(solution)/shard_map/btij,bif->btjf/dot_general | solution.py:45
  242.3 9.3 %convolution_bitcast_fusion = f32[16,256,256]{2,0,1:T(8,128)S(1)} fusion(f32[4,6,256,256]{3,1,0,2:T(8,128)} %copy.19, f32[4,6]{1,0:T(4,128)S(1)} %fusion.18, s32[4,6]{1,0:T(4,128)S(1)} %bitcast.52), kind=kOutput, calls=%fused_computation.9 | convolution fusion | flops 301990656 | bytes 10485952 | tf_op jit(solution)/shard_map/btc,btjf->cjf/dot_general | solution.py:51
  251.6 4.4 copy.20
  255.9 0.0 reduce-scatter.2.cloned.1.call-update
  256.0 55.6 %psum.15 = f32[256]{0:T(256)} all-reduce(f32[256]{0:T(256)S(1)} %broadcast_multiply_fusion), channel_id=1, replica_groups=mesh['grp'=8,'row'=32] {'row'}, use_global_device_ids=true, to_apply=%region_4.0 | all-reduce | flops 256 | bytes 2048 | tf_op jit(solution)/shard_map/psum | solution.py:43
  311.5 135.0 %all-reduce.2.cloned.1.call-done = f32[256,256]{1,0:T(8,128)} async-done(((f32[256,256]{1,0:T(8,128)}), f32[256,256]{1,0:T(8,128)}) %all-reduce.2.cloned.1.call-update) | async-done | bytes 262160 | tf_op jit(solution)/shard_map/psum | solution.py:43
  446.6 128.9 %reduce-scatter.2.cloned.1.call-done = f32[128,256]{1,0:T(8,128)} async-done(((f32[4096,256]{1,0:T(8,128)}), f32[128,256]{1,0:T(8,128)}) %reduce-scatter.2.cloned.1.call-update) | async-done | bytes 131088 | tf_op jit(solution)/shard_map/reduce_scatter | solution.py:54
  575.5 1.7 copy.34
  (7 shorter events, 0.0 us)
Async XLA Ops:
  7.2 207.6 %copy-start = (f32[256,256]{1,0:T(8,128)S(1)}, f32[256,256]{1,0:T(8,128)}, u32[]{:S(2)}) copy-start(f32[256,256]{1,0:T(8,128)} %param.11) | copy-start | bytes 786436
  7.2 72.0 %all-gather.3.cloned.1.call-start = ((), (), s32[]{:S(2)}) async-start(), calls=%async_computation.1 | async-start | bytes 4325376 | tf_op jit(solution)/shard_map/all_gather | solution.py:24
  7.2 83.8 %slice-start = ((s8[6291456]{0:T(1024)(128)(4,1)}), s8[2097152]{0:T(1024)(128)(4,1)S(1)}, s32[]{:S(2)}) async-start(s8[6291456]{0:T(1024)(128)(4,1)} %bitcast.45), calls=%async_computation.5 | async-start | bytes 4194304
  7.9 202.8 %all-gather.5.cloned.1.call-start = ((), (), s32[]{:S(2)}) async-start(), calls=%async_computation.2 | async-start | bytes 9437184 | tf_op jit(solution)/shard_map/all_gather | solution.py:9
  79.2 11.9 %slice-start.1 = ((s8[6291456]{0:T(1024)(128)(4,1)}), s8[4194304]{0:T(1024)(128)(4,1)S(1)}, s32[]{:S(2)}) async-start(s8[6291456]{0:T(1024)(128)(4,1)} %bitcast.45), calls=%async_computation.6 | async-start | bytes 8388608
  100.6 114.2 %copy-start.2 = (f32[1024,256]{1,0:T(8,128)S(1)}, f32[1024,256]{1,0:T(8,128)}, u32[]{:S(2)}) copy-start(f32[1024,256]{1,0:T(8,128)} %param.13) | copy-start | bytes 3145732
  100.6 114.2 %copy-start.3 = (f32[256]{0:T(256)S(1)}, f32[256]{0:T(256)}, u32[]{:S(2)}) copy-start(f32[256]{0:T(256)} %param.12) | copy-start | bytes 3076
  100.6 346.0 %all-reduce.2.cloned.1.call-start = ((), (), s32[]{:S(2)}) async-start(), calls=%async_computation.4 | async-start | bytes 524288 | tf_op jit(solution)/shard_map/psum | solution.py:43
  220.7 354.9 %reduce-scatter.2.cloned.1.call-start = ((), (), s32[]{:S(2)}) async-start(), calls=%async_computation.3 | async-start | bytes 4325376 | tf_op jit(solution)/shard_map/reduce_scatter | solution.py:54
  232.8 9.4 %copy-start.1 = (s32[4,1,6]{2,1,0:T(1,128)S(1)}, s32[4,1,6]{2,1,0:T(1,128)}, u32[]{:S(2)}) copy-start(s32[4,1,6]{2,1,0:T(1,128)} %param.9) | copy-start | bytes 292
Sparse Core Ops, SparseCore 0:
  9.8 69.2 all-gather.2
  100.7 109.9 all-gather.4
  220.8 225.7 all-reduce.1
  449.5 125.9 reduce-scatter.1
